TPU v7x, 32 devices: a whole 2x2x4 slice. The times are simulated.
32 devices in a mesh: rows: 8 (over z, x), rhs: 4 (over y, core).
Axes of the slice: x: 2, y: 2, z: 4, core: 2. Of those that a mesh axis runs over, the one named last changes fastest.
Arguments:
- right_side: float32 [4, 64, 256, 256], P(None, 'rows', 'rhs'), parts along dimension 2, may hold values from -6 to 6
- prior: float32 [64, 256, 256], P('rows', 'rhs'), parts along dimension 1, may hold values from -6 to 6
- lower_blocks: float32 [4, 64, 4, 256, 256], P(None, 'rows'), may hold values from -0.09375 to 0.09375
- inverse_diag: float32 [4, 64, 256, 256], P(None, 'rows'), may hold values from -0.375 to 0.375
- fill_cols: int32 [4, 64, 4], P(None, 'rows'), may hold values from -1 to 255, as said below
Outputs:
- solution: float32 [4, 64, 256, 256], P(None, 'rows', 'rhs'), parts along dimension 2
There are 4 independent parts, one for each index of `rhs`. A program takes and returns all parts, laid end to end along the dimension named above; an argument that names none is the same for every part. Nothing has to cross between parts.
Inputs may be any that keep to these rules, and one draw needn't show every extreme that they name: `fill_cols`: for block row j of level l, held at index d = j // 8 of rows with position k = j % 8: every filled slot names a panel of the level before (the prior panels for l = 0), numbered l * 64 + e * 8 + k2, whose holder e is d, d XOR 2^a or d XOR 2^b, where a = 2l mod log2 of the rows axis size and b = (2l + 1) mod log2 of it. Slot 0 names position k at holder d XOR 2^a, slot 1 position k at holder d XOR 2^b; the further slots name distinct other panels of these three holders, and filled slots come first, followed by -1.
All inputs are finite; a program needn't handle non-finite values.
Results may differ from a plain program's by a relative error of at most 0.0001.
Values sent between devices are 32-bit elements; how exact they have to be, the bound alone decides.
A program may use at most 192 MiB of HBM per device.

v0:
```python
import jax
import jax.numpy as jnp
from jax import lax
from jax.sharding import PartitionSpec as P


def swapped(block, axis, distance):
    count = lax.axis_size(axis)
    route = []
    for low in range(count):
        high = low | 1 << distance
        if high != low and high < count:
            route += [(low, high), (high, low)]
    return lax.ppermute(block, axis, route)


def pick_segments(segment_table, position, filled):
    entries = jnp.arange(segment_table.shape[0], dtype=jnp.int32)
    onehot = ((position[:, :, None] == entries[None, None, :]) & filled[:, :, None]).astype(
        jnp.float32
    )
    return jnp.einsum("jfp,pnc->jfnc", onehot, segment_table, precision=lax.Precision.HIGHEST)


def body(right_side, prior, lower_blocks, inverse_diag, fill_cols):
    highest = lax.Precision.HIGHEST
    level_count = right_side.shape[0]
    per_dev = right_side.shape[1]
    devices = lax.axis_size("rows")
    bit_count = devices.bit_length() - 1
    my_index = lax.axis_index("rows")
    level_rows = devices * per_dev
    previous = prior
    solved = []
    for height in range(level_count):
        columns = fill_cols[height]
        filled = columns >= 0
        relative = columns - height * level_rows
        first_bit = 2 * height % bit_count
        second_bit = (2 * height + 1) % bit_count
        first_rows = swapped(previous, "rows", first_bit)
        second_rows = swapped(previous, "rows", second_bit)
        segment_table = jnp.concatenate([previous, first_rows, second_rows], axis=0)
        holder = relative // per_dev
        within = relative % per_dev
        first_holder = jnp.bitwise_xor(my_index, 1 << first_bit)
        position = jnp.where(
            holder == my_index,
            within,
            jnp.where(holder == first_holder, per_dev + within, 2 * per_dev + within),
        )
        picked = pick_segments(segment_table, position, filled)
        contribution = jnp.einsum("jfnc,jfrc->jnr", picked, lower_blocks[height], precision=highest)
        reduced = right_side[height] - contribution
        current = jnp.einsum("jnc,jrc->jnr", reduced, inverse_diag[height], precision=highest)
        solved.append(current)
        previous = current
    return jnp.stack(solved)


def solution(mesh):
    return jax.shard_map(
        body,
        mesh=mesh,
        in_specs=(
            P(None, "rows", "rhs", None),
            P("rows", "rhs", None),
            P(None, "rows", None, None, None),
            P(None, "rows", None, None),
            P(None, "rows", None),
        ),
        out_specs=P(None, "rows", "rhs", None),
        check_vma=False,
    )
```

profile of v0, /device:TPU:0, one launch (start us, length us, event | category | flops | bytes accessed | tf_op | source)
XLA Modules:
  0.0 152.1 jit_solution(13229651773085961724)
XLA Ops:
  0.0 2.9 %collective-permute-start = (f32[8,64,256]{2,1,0:T(8,128)}, f32[8,64,256]{2,1,0:T(8,128)S(1)}, u32[]{:S(2)}, u32[]{:S(2)}) collective-permute-start(f32[8,64,256]{2,1,0:T(8,128)} %param.6), channel_id=1, source_target_pairs={{0,4},{4,0},{8,12},{12,8},{16,20},{20,16},{24,28},{28,24},{1,5},{5... | collective-permute-start | bytes 1572872 | tf_op jit(solution)/shard_map/ppermute | solution.py:14
  2.9 1.6 %collective-permute-start.1 = (f32[8,64,256]{2,1,0:T(8,128)}, f32[8,64,256]{2,1,0:T(8,128)S(1)}, u32[]{:S(2)}, u32[]{:S(2)}) collective-permute-start(f32[8,64,256]{2,1,0:T(8,128)} %param.6), channel_id=1, source_target_pairs={{0,8},{8,0},{4,12},{12,4},{16,24},{24,16},{20,28},{28,20},{1,9},{9... | collective-permute-start | bytes 1572872 | tf_op jit(solution)/shard_map/ppermute | solution.py:14
  4.5 0.7 bitcast_compare_fusion.3
  5.2 0.1 copy.7
  5.3 0.8 select_select_fusion
  6.1 0.1 copy.6
  6.1 8.9 %collective-permute-done = f32[8,64,256]{2,1,0:T(8,128)S(1)} collective-permute-done((f32[8,64,256]{2,1,0:T(8,128)}, f32[8,64,256]{2,1,0:T(8,128)S(1)}, u32[]{:S(2)}, u32[]{:S(2)}) %collective-permute-start) | collective-permute-done | bytes 524320 | tf_op jit(solution)/shard_map/ppermute | solution.py:14
  15.1 1.5 collective-permute-done.1
  16.5 1.2 maximum_bitcast_fusion
  17.8 0.0 copy-start
  17.8 2.5 %fusion.34 = f32[8,4,64,256]{3,1,2,0:T(4,128)S(1)} fusion(f32[24,64,256,1]{2,1,0,3:T(8,128)S(1)} %maximum_bitcast_fusion, s32[8,4]{1,0:T(8,128)S(1)} %copy.6, pred[8,4]{1,0:T(8,128)(4,1)S(1)} %copy.7), kind=kOutput, calls=%fused_computation.39 | convolution fusion | flops 150996480 | bytes 3670176 | tf_op jit(solution)/shard_map/jfp,pnc->jfnc/dot_general | solution.py:22
  20.3 0.0 copy-done
  20.3 10.6 %fusion.74 = f32[8,64,256]{2,1,0:T(8,128)S(1)} fusion(f32[4,8,4,256,256]{4,3,2,1,0:T(8,128)} %param.7, f32[8,4,64,256]{3,1,2,0:T(4,128)S(1)} %fusion.34, f32[4,8,64,256]{3,2,1,0:T(8,128)S(1)} %copy-done), kind=kOutput, calls=%fused_computation.49 | convolution fusion | flops 1610743808 | bytes 11534336 | tf_op jit(solution)/shard_map/jfnc,jfrc->jnr/dot_general | solution.py:53
  30.9 0.0 copy-start.1
  30.9 3.7 %fusion.18 = f32[8,64,256]{2,1,0:T(8,128)S(1)} fusion(f32[8,64,256]{2,1,0:T(8,128)S(1)} %fusion.74, f32[4,8,256,256]{3,2,1,0:T(8,128)} %param.8), kind=kOutput, calls=%fused_computation.19 | convolution fusion | flops 402653184 | bytes 3145728 | tf_op jit(solution)/shard_map/jnc,jrc->jnr/dot_general | solution.py:55
  34.6 0.5 collective-permute-start.3
  35.1 2.7 %collective-permute-start.2 = (f32[8,64,256]{2,1,0:T(8,128)S(1)}, f32[8,64,256]{2,1,0:T(8,128)}, u32[]{:S(2)}, u32[]{:S(2)}) collective-permute-start(f32[8,64,256]{2,1,0:T(8,128)S(1)} %fusion.18), channel_id=1, source_target_pairs={{0,16},{16,0},{4,20},{20,4},{8,24},{24,8},{12,28},{28,12},{1,17},{... | collective-permute-start | bytes 1572872 | tf_op jit(solution)/shard_map/ppermute | solution.py:14
  37.8 0.0 copy-done.1
  37.8 0.1 copy.9
  37.9 0.1 copy.8
  38.0 9.2 %collective-permute-done.3 = f32[8,64,256]{2,1,0:T(8,128)S(1)} collective-permute-done((f32[8,64,256]{2,1,0:T(8,128)S(1)}, f32[8,64,256]{2,1,0:T(8,128)S(1)}, u32[]{:S(2)}, u32[]{:S(2)}) %collective-permute-start.3) | collective-permute-done | bytes 524320 | tf_op jit(solution)/shard_map/ppermute | solution.py:14
  47.1 12.7 %collective-permute-done.2 = f32[8,64,256]{2,1,0:T(8,128)} collective-permute-done((f32[8,64,256]{2,1,0:T(8,128)S(1)}, f32[8,64,256]{2,1,0:T(8,128)}, u32[]{:S(2)}, u32[]{:S(2)}) %collective-permute-start.2) | collective-permute-done | bytes 524320 | tf_op jit(solution)/shard_map/ppermute | solution.py:14
  59.8 1.2 maximum_bitcast_fusion.1
  61.0 2.5 %fusion.32 = f32[8,4,64,256]{3,1,2,0:T(4,128)S(1)} fusion(f32[24,64,256,1]{2,1,0,3:T(8,128)S(1)} %maximum_bitcast_fusion.1, s32[8,4]{1,0:T(8,128)S(1)} %copy.8, pred[8,4]{1,0:T(8,128)(4,1)S(1)} %copy.9), kind=kOutput, calls=%fused_computation.37 | convolution fusion | flops 150996480 | bytes 3670176 | tf_op jit(solution)/shard_map/jfp,pnc->jfnc/dot_general | solution.py:22
  63.5 10.7 %fusion.69 = f32[8,64,256]{2,1,0:T(8,128)S(1)} fusion(f32[4,8,4,256,256]{4,3,2,1,0:T(8,128)} %param.7, f32[8,4,64,256]{3,1,2,0:T(4,128)S(1)} %fusion.32, f32[4,8,64,256]{3,2,1,0:T(8,128)S(1)} %copy-done), kind=kOutput, calls=%fused_computation.48 | convolution fusion | flops 1610743808 | bytes 11534336 | tf_op jit(solution)/shard_map/jfnc,jfrc->jnr/dot_general | solution.py:53
  74.2 3.7 %fusion.16 = f32[8,64,256]{2,1,0:T(8,128)S(1)} fusion(f32[8,64,256]{2,1,0:T(8,128)S(1)} %fusion.69, f32[4,8,256,256]{3,2,1,0:T(8,128)} %param.8), kind=kOutput, calls=%fused_computation.17 | convolution fusion | flops 402653184 | bytes 3145728 | tf_op jit(solution)/shard_map/jnc,jrc->jnr/dot_general | solution.py:55
  77.9 0.1 collective-permute-start.5
  77.9 3.9 %collective-permute-start.4 = (f32[8,64,256]{2,1,0:T(8,128)S(1)}, f32[8,64,256]{2,1,0:T(8,128)}, u32[]{:S(2)}, u32[]{:S(2)}) collective-permute-start(f32[8,64,256]{2,1,0:T(8,128)S(1)} %fusion.16), channel_id=1, source_target_pairs={{0,8},{8,0},{4,12},{12,4},{16,24},{24,16},{20,28},{28,20},{1,9},{9... | collective-permute-start | bytes 1572872 | tf_op jit(solution)/shard_map/ppermute | solution.py:14
  81.9 0.1 copy.11
  82.0 0.1 copy.10
  82.0 21.1 %collective-permute-done.5 = f32[8,64,256]{2,1,0:T(8,128)} collective-permute-done((f32[8,64,256]{2,1,0:T(8,128)S(1)}, f32[8,64,256]{2,1,0:T(8,128)}, u32[]{:S(2)}, u32[]{:S(2)}) %collective-permute-start.5) | collective-permute-done | bytes 524320 | tf_op jit(solution)/shard_map/ppermute | solution.py:14
  103.2 0.1 collective-permute-done.4
  103.2 1.4 maximum_bitcast_fusion.2
  104.6 2.5 %fusion.30 = f32[8,4,64,256]{3,1,2,0:T(4,128)S(1)} fusion(f32[24,64,256,1]{2,1,0,3:T(8,128)S(1)} %maximum_bitcast_fusion.2, s32[8,4]{1,0:T(8,128)S(1)} %copy.10, pred[8,4]{1,0:T(8,128)(4,1)S(1)} %copy.11), kind=kOutput, calls=%fused_computation.35 | convolution fusion | flops 150996480 | bytes 3670176 | tf_op jit(solution)/shard_map/jfp,pnc->jfnc/dot_general | solution.py:22
  107.1 10.4 %fusion.64 = f32[8,64,256]{2,1,0:T(8,128)S(1)} fusion(f32[4,8,4,256,256]{4,3,2,1,0:T(8,128)} %param.7, f32[8,4,64,256]{3,1,2,0:T(4,128)S(1)} %fusion.30, f32[4,8,64,256]{3,2,1,0:T(8,128)S(1)} %copy-done), kind=kOutput, calls=%fused_computation.47 | convolution fusion | flops 1610743808 | bytes 11534336 | tf_op jit(solution)/shard_map/jfnc,jfrc->jnr/dot_general | solution.py:53
  117.6 3.7 %fusion.14 = f32[8,64,256]{2,1,0:T(8,128)S(1)} fusion(f32[8,64,256]{2,1,0:T(8,128)S(1)} %fusion.64, f32[4,8,256,256]{3,2,1,0:T(8,128)} %param.8), kind=kOutput, calls=%fused_computation.15 | convolution fusion | flops 402653184 | bytes 3145728 | tf_op jit(solution)/shard_map/jnc,jrc->jnr/dot_general | solution.py:55
  121.3 0.1 collective-permute-start.7
  121.3 1.2 collective-permute-start.6
  122.6 0.1 copy.13
  122.7 0.1 copy.12
  122.7 10.5 %collective-permute-done.7 = f32[8,64,256]{2,1,0:T(8,128)S(1)} collective-permute-done((f32[8,64,256]{2,1,0:T(8,128)S(1)}, f32[8,64,256]{2,1,0:T(8,128)S(1)}, u32[]{:S(2)}, u32[]{:S(2)}) %collective-permute-start.7) | collective-permute-done | bytes 524320 | tf_op jit(solution)/shard_map/ppermute | solution.py:14
  133.3 0.1 collective-permute-done.6
  133.3 0.2 maximum_bitcast_fusion.3
  133.5 2.5 %fusion.28 = f32[8,4,64,256]{3,1,2,0:T(4,128)S(1)} fusion(f32[24,64,256,1]{2,1,0,3:T(8,128)S(1)} %maximum_bitcast_fusion.3, s32[8,4]{1,0:T(8,128)S(1)} %copy.12, pred[8,4]{1,0:T(8,128)(4,1)S(1)} %copy.13), kind=kOutput, calls=%fused_computation.33 | convolution fusion | flops 150996480 | bytes 3670176 | tf_op jit(solution)/shard_map/jfp,pnc->jfnc/dot_general | solution.py:22
  136.0 10.9 %fusion.59 = f32[8,64,256]{2,1,0:T(8,128)S(1)} fusion(f32[4,8,4,256,256]{4,3,2,1,0:T(8,128)} %param.7, f32[8,4,64,256]{3,1,2,0:T(4,128)S(1)} %fusion.28, f32[4,8,64,256]{3,2,1,0:T(8,128)} %param.5), kind=kOutput, calls=%fused_computation.46 | convolution fusion | flops 1610743808 | bytes 11534336 | tf_op jit(solution)/shard_map/jfnc,jfrc->jnr/dot_general | solution.py:53
  146.9 3.7 %fusion.36 = f32[1,8,64,256]{3,2,1,0:T(8,128)S(1)} fusion(f32[8,64,256]{2,1,0:T(8,128)S(1)} %fusion.59, f32[4,8,256,256]{3,2,1,0:T(8,128)} %param.8), kind=kOutput, calls=%fused_computation.41 | convolution fusion | flops 402653184 | bytes 3145728 | tf_op jit(solution)/shard_map/jnc,jrc->jnr/dot_general | solution.py:55
  150.6 1.5 pad_maximum_fusion
  (1 shorter events, 0.0 us)
Async XLA Ops:
  0.0 15.1 %collective-permute-start = (f32[8,64,256]{2,1,0:T(8,128)}, f32[8,64,256]{2,1,0:T(8,128)S(1)}, u32[]{:S(2)}, u32[]{:S(2)}) collective-permute-start(f32[8,64,256]{2,1,0:T(8,128)} %param.6), channel_id=1, source_target_pairs={{0,4},{4,0},{8,12},{12,8},{16,20},{20,16},{24,28},{28,24},{1,5},{5... | collective-permute-start | bytes 1572872 | tf_op jit(solution)/shard_map/ppermute | solution.py:14
  2.9 13.6 %collective-permute-start.1 = (f32[8,64,256]{2,1,0:T(8,128)}, f32[8,64,256]{2,1,0:T(8,128)S(1)}, u32[]{:S(2)}, u32[]{:S(2)}) collective-permute-start(f32[8,64,256]{2,1,0:T(8,128)} %param.6), channel_id=1, source_target_pairs={{0,8},{8,0},{4,12},{12,4},{16,24},{24,16},{20,28},{28,20},{1,9},{9... | collective-permute-start | bytes 1572872 | tf_op jit(solution)/shard_map/ppermute | solution.py:14
  17.8 2.5 %copy-start = (f32[4,8,64,256]{3,2,1,0:T(8,128)S(1)}, f32[4,8,64,256]{3,2,1,0:T(8,128)}, u32[]{:S(2)}) copy-start(f32[4,8,64,256]{3,2,1,0:T(8,128)} %param.5) | copy-start | bytes 6291460
  30.9 6.9 %copy-start.1 = (s32[4,8,4]{1,2,0:T(4,128)S(1)}, s32[4,8,4]{1,2,0:T(4,128)}, u32[]{:S(2)}) copy-start(s32[4,8,4]{1,2,0:T(4,128)} %param.9) | copy-start | bytes 1540
  34.6 12.5 %collective-permute-start.3 = (f32[8,64,256]{2,1,0:T(8,128)S(1)}, f32[8,64,256]{2,1,0:T(8,128)S(1)}, u32[]{:S(2)}, u32[]{:S(2)}) collective-permute-start(f32[8,64,256]{2,1,0:T(8,128)S(1)} %fusion.18), channel_id=1, source_target_pairs={{0,4},{4,0},{8,12},{12,8},{16,20},{20,16},{24,28},{28,24},{1,5},{5... | collective-permute-start | bytes 1572872 | tf_op jit(solution)/shard_map/ppermute | solution.py:14
  35.1 24.8 %collective-permute-start.2 = (f32[8,64,256]{2,1,0:T(8,128)S(1)}, f32[8,64,256]{2,1,0:T(8,128)}, u32[]{:S(2)}, u32[]{:S(2)}) collective-permute-start(f32[8,64,256]{2,1,0:T(8,128)S(1)} %fusion.18), channel_id=1, source_target_pairs={{0,16},{16,0},{4,20},{20,4},{8,24},{24,8},{12,28},{28,12},{1,17},{... | collective-permute-start | bytes 1572872 | tf_op jit(solution)/shard_map/ppermute | solution.py:14
  77.9 25.3 %collective-permute-start.5 = (f32[8,64,256]{2,1,0:T(8,128)S(1)}, f32[8,64,256]{2,1,0:T(8,128)}, u32[]{:S(2)}, u32[]{:S(2)}) collective-permute-start(f32[8,64,256]{2,1,0:T(8,128)S(1)} %fusion.16), channel_id=1, source_target_pairs={{0,16},{16,0},{4,20},{20,4},{8,24},{24,8},{12,28},{28,12},{1,17},{... | collective-permute-start | bytes 1572872 | tf_op jit(solution)/shard_map/ppermute | solution.py:14
  77.9 25.3 %collective-permute-start.4 = (f32[8,64,256]{2,1,0:T(8,128)S(1)}, f32[8,64,256]{2,1,0:T(8,128)}, u32[]{:S(2)}, u32[]{:S(2)}) collective-permute-start(f32[8,64,256]{2,1,0:T(8,128)S(1)} %fusion.16), channel_id=1, source_target_pairs={{0,8},{8,0},{4,12},{12,4},{16,24},{24,16},{20,28},{28,20},{1,9},{9... | collective-permute-start | bytes 1572872 | tf_op jit(solution)/shard_map/ppermute | solution.py:14
  121.3 12.0 %collective-permute-start.7 = (f32[8,64,256]{2,1,0:T(8,128)S(1)}, f32[8,64,256]{2,1,0:T(8,128)S(1)}, u32[]{:S(2)}, u32[]{:S(2)}) collective-permute-start(f32[8,64,256]{2,1,0:T(8,128)S(1)} %fusion.14), channel_id=1, source_target_pairs={{0,8},{8,0},{4,12},{12,4},{16,24},{24,16},{20,28},{28,20},{1,9},{9... | collective-permute-start | bytes 1572872 | tf_op jit(solution)/shard_map/ppermute | solution.py:14
  121.3 12.0 %collective-permute-start.6 = (f32[8,64,256]{2,1,0:T(8,128)S(1)}, f32[8,64,256]{2,1,0:T(8,128)S(1)}, u32[]{:S(2)}, u32[]{:S(2)}) collective-permute-start(f32[8,64,256]{2,1,0:T(8,128)S(1)} %fusion.14), channel_id=1, source_target_pairs={{0,4},{4,0},{8,12},{12,8},{16,20},{20,16},{24,28},{28,24},{1,5},{5... | collective-permute-start | bytes 1572872 | tf_op jit(solution)/shard_map/ppermute | solution.py:14
where the time goes:
time: 153 us; the launch traced here: 152 us
  matrix products  67.4 us (44%)
  waiting for transfers between devices  64 us (42%)
  starting transfers between devices  13 us (8%)
  other arithmetic  6.84 us (4%)
    ppermute x8, waiting for transfers between devices, swapped(): return lax.ppermute(block, axis, route)  64 us
    dot_general x4, matrix products, body(): jnp.einsum('jfnc,jfrc->jnr', picked, lower_blocks[height], precision=high...  42.6 us
    dot_general x4, matrix products, body(): jnp.einsum('jnc,jrc->jnr', reduced, inverse_diag[height], precision=highest)  14.7 us
    ppermute x8, starting transfers between devices, swapped(): return lax.ppermute(block, axis, route)  13 us
    dot_general x4, matrix products, pick_segments(): jnp.einsum('jfp,pnc->jfnc', onehot, segment_table, precision=lax.Precisio...  10.1 us
    concatenate x4, other arithmetic, body(): segment_table = jnp.concatenate([previous, first_rows, second_rows], axis=0)  3.91 us
  transfers between devices with their start and end apart: 8, of which 8 were waited for; matrix products, arithmetic and copies ran while one was open for 1% of the time, Pallas kernels for 0%

commit v1 on v0

v1 whole, which is shorter than its diff:
```python
import functools

import jax
import jax.numpy as jnp
from jax import lax
from jax.experimental import pallas as pl
from jax.experimental.pallas import tpu as pltpu
from jax.sharding import PartitionSpec as P

CHUNKS = 2
STAGE = 6
KEPT = 3


def split(x):
    high = x.astype(jnp.bfloat16)
    low = (x - high.astype(jnp.float32)).astype(jnp.bfloat16)
    return high, low


def times_transposed(left, right):
    return lax.dot_general(
        left, right, (((1,), (1,)), ((), ())), preferred_element_type=jnp.float32
    )


def product(panel, high, low):
    count = panel.shape[0]
    panel_high, panel_low = split(panel)
    both = times_transposed(jnp.concatenate([panel_high, panel_low], axis=0), high)
    return both[:count] + both[count:] + times_transposed(panel_high, low)


def kernel(
    right_hbm, prior_hbm, lower_hbm, inverse_hbm, fill, out_hbm,
    tables, last, right, stage, high_blocks, low_blocks,
    stage_sem, right_sem, prior_sem, send_sem, recv_sem, out_sem,
):
    levels, per_dev, fills = fill.shape
    devices = lax.axis_size("rows")
    bits = devices.bit_length() - 1
    me = lax.axis_index("rows")
    width = right.shape[2] // CHUNKS
    units = levels * per_dev
    partners = [
        [jnp.bitwise_xor(me, 1 << (2 * l + j) % bits) for j in range(2)] for l in range(levels)
    ]

    def stage_copies(unit):
        level, row, slot = unit // per_dev, unit % per_dev, unit % STAGE
        return (
            pltpu.make_async_copy(
                lower_hbm.at[level, row], stage.at[slot, pl.ds(0, fills)], stage_sem.at[0, slot]
            ),
            pltpu.make_async_copy(
                inverse_hbm.at[level, row], stage.at[slot, fills], stage_sem.at[1, slot]
            ),
        )

    def rows_of(c):
        return pl.ds(c * width, width)

    def prior_send(c, j):
        return pltpu.make_async_remote_copy(
            src_ref=prior_hbm.at[:, rows_of(c)],
            dst_ref=tables[0][c].at[pl.ds((j + 1) * per_dev, per_dev)],
            send_sem=send_sem.at[0, c, j],
            recv_sem=recv_sem.at[0, c, j],
            device_id={"rows": partners[0][j]},
            device_id_type=pl.DeviceIdType.MESH,
        )

    def panel_send(l, c, j, first, count):
        table = tables[l][c]
        return pltpu.make_async_remote_copy(
            src_ref=table.at[pl.ds(first, count)],
            dst_ref=table.at[pl.ds((j + 1) * per_dev + first, count)],
            send_sem=send_sem.at[l, c, j],
            recv_sem=recv_sem.at[l, c, j],
            device_id={"rows": partners[l][j]},
            device_id_type=pl.DeviceIdType.MESH,
        )

    def solved(l, c):
        return last[c] if l == levels - 1 else tables[l + 1][c].at[pl.ds(0, per_dev)]

    def out_copy(l, c):
        return pltpu.make_async_copy(
            solved(l, c), out_hbm.at[l, :, rows_of(c)], out_sem.at[l, c]
        )

    def prior_copy(c):
        return pltpu.make_async_copy(
            prior_hbm.at[:, rows_of(c)], tables[0][c].at[pl.ds(0, per_dev)], prior_sem.at[c]
        )

    def right_copy(l):
        return pltpu.make_async_copy(right_hbm.at[l], right.at[l], right_sem.at[l])

    def convert(level):
        kept = level % KEPT

        def one(row, carry):
            unit = level * per_dev + row
            slot = unit % STAGE
            for copy in stage_copies(unit):
                copy.wait()

            def block(b, inner):
                high, low = split(stage[slot, b])
                high_blocks[kept, row, b] = high
                low_blocks[kept, row, b] = low
                return inner

            lax.fori_loop(0, fills + 1, block, 0)

            @pl.when(unit + STAGE < units)
            def _():
                for copy in stage_copies(unit + STAGE):
                    copy.start()

            return carry

        lax.fori_loop(0, per_dev, one, 0)

    def step(l, c):
        kept = l % KEPT
        if l == 0:
            prior_copy(c).wait()
        if c == 0:
            right_copy(l).wait()
        for j in range(2):
            panel_send(l, c, j, 0, per_dev).wait_recv()
        table = tables[l][c]

        def one(row, carry):
            total = jnp.zeros((width, right.shape[3]), jnp.float32)
            for f in range(fills):
                column = fill[l, row, f]
                relative = jnp.maximum(column - l * devices * per_dev, 0)
                holder, within = relative // per_dev, relative % per_dev
                group = jnp.where(
                    holder == me, 0, jnp.where(holder == partners[l][0], 1, 2)
                )
                filled = jnp.where(column >= 0, 1.0, 0.0).astype(jnp.float32)
                panel = table[group * per_dev + within] * filled
                total += product(panel, high_blocks[kept, row, f], low_blocks[kept, row, f])
            reduced = right[l, row, rows_of(c)] - total
            current = product(
                reduced, high_blocks[kept, row, fills], low_blocks[kept, row, fills]
            )
            if l == levels - 1:
                last[c][row] = current
            else:
                tables[l + 1][c][row] = current
                for j in range(2):
                    panel_send(l + 1, c, j, row, 1).start()
            return carry

        lax.fori_loop(0, per_dev, one, 0)
        out_copy(l, c).start()

    for unit in range(min(STAGE, units)):
        for copy in stage_copies(unit):
            copy.start()
    for c in range(CHUNKS):
        prior_copy(c).start()
    for l in range(levels):
        right_copy(l).start()

    barrier = pltpu.get_barrier_semaphore()
    for bit in range(bits):
        pl.semaphore_signal(
            barrier,
            inc=1,
            device_id={"rows": jnp.bitwise_xor(me, 1 << bit)},
            device_id_type=pl.DeviceIdType.MESH,
        )
    pl.semaphore_wait(barrier, bits)

    for c in range(CHUNKS):
        for j in range(2):
            prior_send(c, j).start()
    for level in range(min(2, levels)):
        convert(level)
    for l in range(levels):
        for c in range(CHUNKS):
            step(l, c)
            if l == 0 and c == 0 and levels > 2:
                convert(2)
        if l + 3 < levels:
            convert(l + 3)
    for c in range(CHUNKS):
        for j in range(2):
            prior_send(c, j).wait_send()
            for l in range(1, levels):
                panel_send(l, c, j, 0, per_dev).wait_send()
        for l in range(levels):
            out_copy(l, c).wait()


def body(right_side, prior, lower_blocks, inverse_diag, fill_cols):
    levels, per_dev, rhs, order = right_side.shape
    fills = fill_cols.shape[2]
    width = rhs // CHUNKS
    f32 = jnp.float32
    dma = pltpu.SemaphoreType.DMA
    any_space = pl.BlockSpec(memory_space=pl.ANY)
    return pl.pallas_call(
        kernel,
        out_shape=jax.ShapeDtypeStruct(right_side.shape, f32),
        in_specs=[any_space] * 4 + [pl.BlockSpec(memory_space=pltpu.SMEM)],
        out_specs=any_space,
        scratch_shapes=[
            [
                [pltpu.VMEM((3 * per_dev, width, order), f32) for _ in range(CHUNKS)]
                for _ in range(levels)
            ],
            [pltpu.VMEM((per_dev, width, order), f32) for _ in range(CHUNKS)],
            pltpu.VMEM(right_side.shape, f32),
            pltpu.VMEM((STAGE, fills + 1, order, order), f32),
            pltpu.VMEM((KEPT, per_dev, fills + 1, order, order), jnp.bfloat16),
            pltpu.VMEM((KEPT, per_dev, fills + 1, order, order), jnp.bfloat16),
            dma((2, STAGE)),
            dma((levels,)),
            dma((CHUNKS,)),
            dma((levels, CHUNKS, 2)),
            dma((levels, CHUNKS, 2)),
            dma((levels, CHUNKS)),
        ],
        compiler_params=pltpu.CompilerParams(
            collective_id=0, has_side_effects=True, vmem_limit_bytes=60 << 20
        ),
    )(right_side, prior, lower_blocks, inverse_diag, fill_cols)


def solution(mesh):
    return jax.shard_map(
        body,
        mesh=mesh,
        in_specs=(
            P(None, "rows", "rhs", None),
            P("rows", "rhs", None),
            P(None, "rows", None, None, None),
            P(None, "rows", None, None),
            P(None, "rows", None),
        ),
        out_specs=P(None, "rows", "rhs", None),
        check_vma=False,
    )
```

time: 153 us -> 83.7 us (0.55)
  Pallas kernels: 0 us -> 78.8 us
  matrix products: 67.4 us -> 0 us
  waiting for transfers between devices: 64 us -> 0 us
  starting transfers between devices: 13 us -> 0 us
  other arithmetic: 6.84 us -> 0 us
  local copies, waits for them, and re-layouts: 0.72 us -> 4.52 us
    pallas_call x0 -> x1, Pallas kernels: none -> 78.8 us  [body(): pl.pallas_call(kernel, out_shape=jax.ShapeDtypeStruct(right_side.shape, f...]
    dot_general x12 -> x0, matrix products: 67.4 us -> none  [the longest x4 42.6 us: body(): jnp.einsum('jfnc,jfrc->jnr', picked, lower_blocks[height], precision=high...]
    ppermute x8 -> x0, waiting for transfers between devices: 64 us -> none  [swapped(): return lax.ppermute(block, axis, route)]
    ppermute x8 -> x0, starting transfers between devices: 13 us -> none  [swapped(): return lax.ppermute(block, axis, route)]
    unnamed x4 -> x2, local copies, waits for them, and re-layouts: 0.01 us -> 4.52 us
    concatenate x4 -> x0, other arithmetic: 3.91 us -> none  [body(): segment_table = jnp.concatenate([previous, first_rows, second_rows], axis=0)]
  transfers between devices with their start and end apart: 8 -> 0, of which waited for: 8 -> 0; matrix products, arithmetic and copies ran while one was open for 1% -> 0% of each run, Pallas kernels for 0% -> 0%
where the time goes in v1:
time: 83.7 us; the launch traced here: 83.4 us
  Pallas kernels  78.8 us (94%)
  local copies, waits for them, and re-layouts  4.52 us (5%)
    pallas_call x1, Pallas kernels, body(): pl.pallas_call(kernel, out_shape=jax.ShapeDtypeStruct(right_side.shape, f...  78.8 us
    unnamed x2, local copies, waits for them, and re-layouts  4.52 us

profile of v1, /device:TPU:0, one launch (start us, length us, event | category | flops | bytes accessed | tf_op | source)
XLA Modules:
  0.0 83.4 jit_solution(2624171753325656214)
XLA Ops:
  0.0 1.4 %copy.6.fill = s32[4,8,4]{2,1,0:T(8,128)} copy(s32[4,8,4]{1,2,0:T(4,128)} %param.9) | data formatting | bytes 1024 | tf_op args[4]
  1.4 78.8 %shard_map.55 = f32[4,8,64,256]{3,2,1,0:T(8,128)} custom-call(f32[4,8,64,256]{3,2,1,0:T(8,128)} %right_hbm.1, f32[8,64,256]{2,1,0:T(8,128)} %prior_hbm.1, f32[4,8,4,256,256]{4,3,2,1,0:T(8,128)} %lower_hbm.1, f32[4,8,256,256]{3,2,1,0:T(8,128)} %inverse_hbm.1, s32[4,8,4]{2,1,0:T(8,128)} %copy.6.fill), custom_call_target="tpu_custom_call" | custom-call | tf_op jit(solution)/shard_map/pallas_call | solution.py:209
  80.2 3.1 %copy.8 = f32[4,8,64,256]{3,2,1,0:T(8,128)} copy(f32[4,8,64,256]{3,2,1,0:T(8,128)} %shard_map.55) | data formatting | bytes 4194304

commit v2 on v1

--- a/solution.py
+++ b/solution.py
@@ -8,8 +8,8 @@
 from jax.sharding import PartitionSpec as P
 
 CHUNKS = 2
-STAGE = 6
-KEPT = 3
+STAGE = 16
+KEPT = 2
 
 
 def split(x):
@@ -18,23 +18,20 @@
     return high, low
 
 
-def times_transposed(left, right):
-    return lax.dot_general(
-        left, right, (((1,), (1,)), ((), ())), preferred_element_type=jnp.float32
-    )
-
-
 def product(panel, high, low):
     count = panel.shape[0]
     panel_high, panel_low = split(panel)
-    both = times_transposed(jnp.concatenate([panel_high, panel_low], axis=0), high)
-    return both[:count] + both[count:] + times_transposed(panel_high, low)
+    both = jnp.dot(
+        jnp.concatenate([panel_high, panel_low], axis=0), high, preferred_element_type=jnp.float32
+    )
+    cross = jnp.dot(panel_high, low, preferred_element_type=jnp.float32)
+    return both[:count] + both[count:] + cross
 
 
 def kernel(
-    right_hbm, prior_hbm, lower_hbm, inverse_hbm, fill, out_hbm,
-    tables, last, right, stage, high_blocks, low_blocks,
-    stage_sem, right_sem, prior_sem, send_sem, recv_sem, out_sem,
+    right_hbm, prior_hbm, lower_hbm, inverse_hbm, fill_hbm, out_hbm,
+    fill, tables, last, right, stage, high_blocks, low_blocks,
+    fill_sem, stage_sem, right_sem, prior_sem, send_sem, recv_sem, out_sem,
 ):
     levels, per_dev, fills = fill.shape
     devices = lax.axis_size("rows")
@@ -107,7 +104,7 @@
                 copy.wait()
 
             def block(b, inner):
-                high, low = split(stage[slot, b])
+                high, low = split(stage[slot, b].T)
                 high_blocks[kept, row, b] = high
                 low_blocks[kept, row, b] = low
                 return inner
@@ -134,7 +131,7 @@
         table = tables[l][c]
 
         def one(row, carry):
-            total = jnp.zeros((width, right.shape[3]), jnp.float32)
+            panels = []
             for f in range(fills):
                 column = fill[l, row, f]
                 relative = jnp.maximum(column - l * devices * per_dev, 0)
@@ -143,8 +140,13 @@
                     holder == me, 0, jnp.where(holder == partners[l][0], 1, 2)
                 )
                 filled = jnp.where(column >= 0, 1.0, 0.0).astype(jnp.float32)
-                panel = table[group * per_dev + within] * filled
-                total += product(panel, high_blocks[kept, row, f], low_blocks[kept, row, f])
+                panels.append(table[group * per_dev + within] * filled)
+            order = right.shape[3]
+            total = product(
+                jnp.concatenate(panels, axis=1),
+                high_blocks[kept, row, :fills].reshape(fills * order, order),
+                low_blocks[kept, row, :fills].reshape(fills * order, order),
+            )
             reduced = right[l, row, rows_of(c)] - total
             current = product(
                 reduced, high_blocks[kept, row, fills], low_blocks[kept, row, fills]
@@ -160,6 +162,8 @@
         lax.fori_loop(0, per_dev, one, 0)
         out_copy(l, c).start()
 
+    fill_copy = pltpu.make_async_copy(fill_hbm, fill, fill_sem)
+    fill_copy.start()
     for unit in range(min(STAGE, units)):
         for copy in stage_copies(unit):
             copy.start()
@@ -181,15 +185,15 @@
     for c in range(CHUNKS):
         for j in range(2):
             prior_send(c, j).start()
-    for level in range(min(2, levels)):
-        convert(level)
+    fill_copy.wait()
+    convert(0)
     for l in range(levels):
         for c in range(CHUNKS):
             step(l, c)
-            if l == 0 and c == 0 and levels > 2:
-                convert(2)
-        if l + 3 < levels:
-            convert(l + 3)
+            if l == 0 and c == 0 and levels > 1:
+                convert(1)
+        if l + KEPT < levels:
+            convert(l + KEPT)
     for c in range(CHUNKS):
         for j in range(2):
             prior_send(c, j).wait_send()
@@ -209,9 +213,10 @@
     return pl.pallas_call(
         kernel,
         out_shape=jax.ShapeDtypeStruct(right_side.shape, f32),
-        in_specs=[any_space] * 4 + [pl.BlockSpec(memory_space=pltpu.SMEM)],
+        in_specs=[any_space] * 5,
         out_specs=any_space,
         scratch_shapes=[
+            pltpu.SMEM(fill_cols.shape, jnp.int32),
             [
                 [pltpu.VMEM((3 * per_dev, width, order), f32) for _ in range(CHUNKS)]
                 for _ in range(levels)
@@ -221,6 +226,7 @@
             pltpu.VMEM((STAGE, fills + 1, order, order), f32),
             pltpu.VMEM((KEPT, per_dev, fills + 1, order, order), jnp.bfloat16),
             pltpu.VMEM((KEPT, per_dev, fills + 1, order, order), jnp.bfloat16),
+            dma,
             dma((2, STAGE)),
             dma((levels,)),
             dma((CHUNKS,)),

time: 83.7 us -> 80.5 us (0.962)
  Pallas kernels: 78.8 us -> 75.8 us
    pallas_call x1, Pallas kernels: 78.8 us -> 75.8 us  [body(): pl.pallas_call(kernel, out_shape=jax.ShapeDtypeStruct(right_side.shape, f...]
where the time goes in v2:
time: 80.5 us; the launch traced here: 80.3 us
  Pallas kernels  75.8 us (94%)
  local copies, waits for them, and re-layouts  4.52 us (6%)
    pallas_call x1, Pallas kernels, body(): pl.pallas_call(kernel, out_shape=jax.ShapeDtypeStruct(right_side.shape, f...  75.8 us
    unnamed x2, local copies, waits for them, and re-layouts  4.52 us

profile of v2, /device:TPU:0, one launch (start us, length us, event | category | flops | bytes accessed | tf_op | source)
XLA Modules:
  0.0 80.3 jit_solution(6421906262809601630)
XLA Ops:
  0.0 1.4 %copy.6.fill_hbm = s32[4,8,4]{2,1,0:T(8,128)} copy(s32[4,8,4]{1,2,0:T(4,128)} %param.9) | data formatting | bytes 1024 | tf_op args[4]
  1.4 75.8 %shard_map.55 = f32[4,8,64,256]{3,2,1,0:T(8,128)} custom-call(f32[4,8,64,256]{3,2,1,0:T(8,128)} %right_hbm.1, f32[8,64,256]{2,1,0:T(8,128)} %prior_hbm.1, f32[4,8,4,256,256]{4,3,2,1,0:T(8,128)} %lower_hbm.1, f32[4,8,256,256]{3,2,1,0:T(8,128)} %inverse_hbm.1, s32[4,8,4]{2,1,0:T(8,128)} %copy.6.fill_hbm), custom_call_target="tpu_custom_call" | custom-call | tf_op jit(solution)/shard_map/pallas_call | solution.py:213
  77.2 3.1 %copy.8 = f32[4,8,64,256]{3,2,1,0:T(8,128)} copy(f32[4,8,64,256]{3,2,1,0:T(8,128)} %shard_map.55) | data formatting | bytes 4194304

commit v3 on v2

--- a/solution.py
+++ b/solution.py
@@ -109,7 +109,7 @@
                 low_blocks[kept, row, b] = low
                 return inner
 
-            lax.fori_loop(0, fills + 1, block, 0)
+            lax.fori_loop(0, fills + 1, block, 0, unroll=5)
 
             @pl.when(unit + STAGE < units)
             def _():
@@ -190,10 +190,10 @@
     for l in range(levels):
         for c in range(CHUNKS):
             step(l, c)
-            if l == 0 and c == 0 and levels > 1:
-                convert(1)
-        if l + KEPT < levels:
-            convert(l + KEPT)
+            if l > 0 and c == 0 and l + 1 < levels:
+                convert(l + 1)
+        if l == 0 and levels > 1:
+            convert(1)
     for c in range(CHUNKS):
         for j in range(2):
             prior_send(c, j).wait_send()

time: 80.5 us -> 77.8 us (0.966)
  Pallas kernels: 75.8 us -> 73.1 us
    pallas_call x1, Pallas kernels: 75.8 us -> 73.1 us  [body(): pl.pallas_call(kernel, out_shape=jax.ShapeDtypeStruct(right_side.shape, f...]
where the time goes in v3:
time: 77.8 us; the launch traced here: 77.6 us
  Pallas kernels  73.1 us (94%)
  local copies, waits for them, and re-layouts  4.52 us (6%)
    pallas_call x1, Pallas kernels, body(): pl.pallas_call(kernel, out_shape=jax.ShapeDtypeStruct(right_side.shape, f...  73.1 us
    unnamed x2, local copies, waits for them, and re-layouts  4.52 us

profile of v3, /device:TPU:0, one launch (start us, length us, event | category | flops | bytes accessed | tf_op | source)
XLA Modules:
  0.0 77.6 jit_solution(11435758282919231144)
XLA Ops:
  0.0 1.4 %copy.6.fill_hbm = s32[4,8,4]{2,1,0:T(8,128)} copy(s32[4,8,4]{1,2,0:T(4,128)} %param.9) | data formatting | bytes 1024 | tf_op args[4]
  1.4 73.1 %shard_map.55 = f32[4,8,64,256]{3,2,1,0:T(8,128)} custom-call(f32[4,8,64,256]{3,2,1,0:T(8,128)} %right_hbm.1, f32[8,64,256]{2,1,0:T(8,128)} %prior_hbm.1, f32[4,8,4,256,256]{4,3,2,1,0:T(8,128)} %lower_hbm.1, f32[4,8,256,256]{3,2,1,0:T(8,128)} %inverse_hbm.1, s32[4,8,4]{2,1,0:T(8,128)} %copy.6.fill_hbm), custom_call_target="tpu_custom_call" | custom-call | tf_op jit(solution)/shard_map/pallas_call | solution.py:213
  74.5 3.1 %copy.8 = f32[4,8,64,256]{3,2,1,0:T(8,128)} copy(f32[4,8,64,256]{3,2,1,0:T(8,128)} %shard_map.55) | data formatting | bytes 4194304

commit v4 on v3

--- a/solution.py
+++ b/solution.py
@@ -153,6 +153,9 @@
             )
             if l == levels - 1:
                 last[c][row] = current
+                pltpu.make_async_copy(
+                    last[c].at[row], out_hbm.at[l, row, rows_of(c)], out_sem.at[l, c]
+                ).start()
             else:
                 tables[l + 1][c][row] = current
                 for j in range(2):
@@ -160,17 +163,8 @@
             return carry
 
         lax.fori_loop(0, per_dev, one, 0)
-        out_copy(l, c).start()
-
-    fill_copy = pltpu.make_async_copy(fill_hbm, fill, fill_sem)
-    fill_copy.start()
-    for unit in range(min(STAGE, units)):
-        for copy in stage_copies(unit):
-            copy.start()
-    for c in range(CHUNKS):
-        prior_copy(c).start()
-    for l in range(levels):
-        right_copy(l).start()
+        if l < levels - 1:
+            out_copy(l, c).start()
 
     barrier = pltpu.get_barrier_semaphore()
     for bit in range(bits):
@@ -180,11 +174,23 @@
             device_id={"rows": jnp.bitwise_xor(me, 1 << bit)},
             device_id_type=pl.DeviceIdType.MESH,
         )
+    fill_copy = pltpu.make_async_copy(fill_hbm, fill, fill_sem)
+    fill_copy.start()
+    for c in range(CHUNKS):
+        prior_copy(c).start()
+    for l in range(levels):
+        right_copy(l).start()
+    for unit in range(min(per_dev, units)):
+        for copy in stage_copies(unit):
+            copy.start()
     pl.semaphore_wait(barrier, bits)
 
     for c in range(CHUNKS):
         for j in range(2):
             prior_send(c, j).start()
+    for unit in range(min(per_dev, units), min(STAGE, units)):
+        for copy in stage_copies(unit):
+            copy.start()
     fill_copy.wait()
     convert(0)
     for l in range(levels):

time: 77.8 us -> 77.7 us (level)
  no operation moved by 1% of the time
where the time goes in v4:
time: 77.7 us; the launch traced here: 77.5 us
  Pallas kernels  72.9 us (94%)
  local copies, waits for them, and re-layouts  4.52 us (6%)
    pallas_call x1, Pallas kernels, body(): pl.pallas_call(kernel, out_shape=jax.ShapeDtypeStruct(right_side.shape, f...  72.9 us
    unnamed x2, local copies, waits for them, and re-layouts  4.52 us

profile of v4, /device:TPU:0, one launch (start us, length us, event | category | flops | bytes accessed | tf_op | source)
XLA Modules:
  0.0 77.5 jit_solution(1095162166952234809)
XLA Ops:
  0.0 1.4 %copy.6.fill_hbm = s32[4,8,4]{2,1,0:T(8,128)} copy(s32[4,8,4]{1,2,0:T(4,128)} %param.9) | data formatting | bytes 1024 | tf_op args[4]
  1.4 72.9 %shard_map.55 = f32[4,8,64,256]{3,2,1,0:T(8,128)} custom-call(f32[4,8,64,256]{3,2,1,0:T(8,128)} %right_hbm.1, f32[8,64,256]{2,1,0:T(8,128)} %prior_hbm.1, f32[4,8,4,256,256]{4,3,2,1,0:T(8,128)} %lower_hbm.1, f32[4,8,256,256]{3,2,1,0:T(8,128)} %inverse_hbm.1, s32[4,8,4]{2,1,0:T(8,128)} %copy.6.fill_hbm), custom_call_target="tpu_custom_call" | custom-call | tf_op jit(solution)/shard_map/pallas_call | solution.py:219
  74.3 3.1 %copy.8 = f32[4,8,64,256]{3,2,1,0:T(8,128)} copy(f32[4,8,64,256]{3,2,1,0:T(8,128)} %shard_map.55) | data formatting | bytes 4194304
